TPU v7x, 128 devices: a whole 4x4x4 slice. The times are simulated.
128 devices in a mesh: dp: 16 (over x_lo, z, core), seq: 8 (over x_hi, y).
Axes of the slice: x: 4 (x_hi: 2, x_lo: 2; x = x_hi * 2 + x_lo), y: 4, z: 4, core: 2. Of those that a mesh axis runs over, the one named last changes fastest.
Arguments:
- video: bfloat16 [16, 8, 256, 1152], P('dp', 'seq'), may hold values from -6 to 6
- out_grad: bfloat16 [16, 8, 256, 1152], P('dp', 'seq'), may hold values from -6 to 6
- gain_spatial: float32 [1152], replicated, may hold values from 0.1 to 1.9
- gain_temporal: float32 [1152], replicated, may hold values from 0.1 to 1.9
- w_spatial_qkv: bfloat16 [1152, 3456], replicated, may hold values from -4 to 4
- w_spatial_out: bfloat16 [1152, 1152], replicated, may hold values from -0.1875 to 0.1875
- w_temporal_qkv: bfloat16 [1152, 3456], replicated, may hold values from -4 to 4
- w_temporal_out: bfloat16 [1152, 1152], replicated, may hold values from -0.1875 to 0.1875
Outputs:
- video_grad: bfloat16 [16, 8, 256, 1152], P('dp', 'seq')
- w_grad: float32 [1152, 1152], P(('dp', 'seq'))
All inputs are finite; a program needn't handle non-finite values.
Results may differ from a plain program's by a relative error of at most 0.018.
Values may be sent and summed in bfloat16 or wider, within the bound.
No kernel may reach another device: no remote copies, remote signals or barrier semaphores. Data moves between devices by JAX's collectives and lax.ppermute only.
A program may use at most 128 MiB of HBM per device.

v0:
```python
import math
import jax
import jax.numpy as jnp
from jax import lax
from jax.sharding import PartitionSpec as P

HEADS = 16
epsilon = 1e-06


def layer_norm(stream, gain_vec):
    center = jnp.mean(stream, axis=-1, keepdims=True)
    centered = stream - center
    spread = jnp.mean(centered * centered, axis=-1, keepdims=True)
    return (centered * lax.rsqrt(spread + epsilon) * gain_vec).astype(jnp.bfloat16)


def project(hidden, weight):
    return jnp.dot(hidden, weight, preferred_element_type=jnp.float32)


def split_heads(block):
    shape = block.shape[:-1] + (HEADS, block.shape[-1] // HEADS)
    return block.reshape(shape).astype(jnp.float32)


def spatial_mix(qkv):
    width = qkv.shape[-1] // 3
    query_part = split_heads(qkv[..., :width])
    key_part = split_heads(qkv[..., width : 2 * width])
    value_part = split_heads(qkv[..., 2 * width :])
    scale = 1.0 / math.sqrt(width // HEADS)
    scores = (
        jnp.einsum("bfqhd,bfkhd->bfhqk", query_part, key_part, precision=lax.Precision.HIGHEST)
        * scale
    )
    weights = jax.nn.softmax(scores, axis=-1)
    mixed = jnp.einsum("bfhqk,bfkhd->bfqhd", weights, value_part, precision=lax.Precision.HIGHEST)
    return mixed.reshape(qkv.shape[:-1] + (width,)).astype(jnp.bfloat16)


def temporal_mix(qkv):
    width = qkv.shape[-1] // 3
    query_part = split_heads(qkv[..., :width])
    key_part = split_heads(qkv[..., width : 2 * width])
    value_part = split_heads(qkv[..., 2 * width :])
    scale = 1.0 / math.sqrt(width // HEADS)
    scores = (
        jnp.einsum("bqphd,bkphd->bphqk", query_part, key_part, precision=lax.Precision.HIGHEST)
        * scale
    )
    weights = jax.nn.softmax(scores, axis=-1)
    mixed = jnp.einsum("bphqk,bkphd->bqphd", weights, value_part, precision=lax.Precision.HIGHEST)
    return mixed.reshape(qkv.shape[:-1] + (width,)).astype(jnp.bfloat16)


def spatial_section(clip, gain_vec, w_qkv, w_out):
    hidden = layer_norm(clip.astype(jnp.float32), gain_vec)
    qkv = project(hidden, w_qkv).astype(jnp.bfloat16)
    return clip.astype(jnp.float32) + project(spatial_mix(qkv), w_out)


def token_outer(mixed, grad_rows):
    width = mixed.shape[-1]
    return lax.dot_general(
        mixed.reshape(-1, width),
        grad_rows.reshape(-1, width),
        (((0,), (0,)), ((), ())),
        preferred_element_type=jnp.float32,
    )


def per_device(
    video,
    out_grad,
    gain_spatial,
    gain_temporal,
    w_spatial_qkv,
    w_spatial_out,
    w_temporal_qkv,
    w_temporal_out,
):
    token_total = (
        lax.axis_size("dp")
        * lax.axis_size("seq")
        * video.shape[0]
        * video.shape[1]
        * video.shape[2]
    )
    stream, spatial_back = jax.vjp(
        lambda clip_in: spatial_section(clip_in, gain_spatial, w_spatial_qkv, w_spatial_out), video
    )
    grad_float = out_grad.astype(jnp.float32)
    qkv, pre_back = jax.vjp(
        lambda stream_in: project(layer_norm(stream_in, gain_temporal), w_temporal_qkv).astype(
            jnp.bfloat16
        ),
        stream,
    )
    moved_qkv = lax.all_to_all(qkv, "seq", split_axis=2, concat_axis=1, tiled=True)
    mixed_pos, mix_back = jax.vjp(temporal_mix, moved_qkv)
    mixed = lax.all_to_all(mixed_pos, "seq", split_axis=1, concat_axis=2, tiled=True)
    local_sum = token_outer(mixed, out_grad)
    unused, out_back = jax.vjp(lambda mixed_in: project(mixed_in, w_temporal_out), mixed)
    mixed_grad = out_back(grad_float)[0]
    mixed_grad_pos = lax.all_to_all(mixed_grad, "seq", split_axis=2, concat_axis=1, tiled=True)
    qkv_grad_pos = mix_back(mixed_grad_pos)[0]
    qkv_grad = lax.all_to_all(qkv_grad_pos, "seq", split_axis=1, concat_axis=2, tiled=True)
    stream_grad = grad_float + pre_back(qkv_grad)[0]
    video_grad = spatial_back(stream_grad)[0]
    local_sum = local_sum / math.sqrt(float(token_total))
    w_grad = lax.psum_scatter(local_sum, ("dp", "seq"), scatter_dimension=0, tiled=True)
    return (video_grad, w_grad)


def solution(mesh):
    return jax.shard_map(
        per_device,
        mesh=mesh,
        in_specs=(
            P("dp", "seq", None, None),
            P("dp", "seq", None, None),
            P(),
            P(),
            P(),
            P(),
            P(),
            P(),
        ),
        out_specs=(P("dp", "seq", None, None), P(("dp", "seq"), None)),
        check_vma=False,
    )
```

profile of v0, /device:TPU:1, one launch (start us, length us, event | category | flops | bytes accessed | tf_op | source)
XLA Modules:
  0.0 361.7 jit_solution(15675530483380894013)
XLA Ops:
  7.2 3.1 fusion.7
  12.8 6.0 %reduce.23 = bf16[256,1152]{1,0:T(8,128)(2,1)} reduce(bf16[256,1,1,1152]{3,2,1,0:T(2,128)(2,1)} %bitcast.153, bf16[]{:T(256)} %broadcast.212), dimensions={1,2}, to_apply=%bitcast.145.reduce_sub_computation | reduce | bytes 1179650
  18.9 2.6 reshape.406
  21.4 7.7 %all-to-all-start = ((bf16[8,2,18432]{2,1,0:T(2,128)(2,1)}), bf16[8,2,18432]{2,1,0:T(2,128)(2,1)}, u32[]{:S(2)}, u32[]{:S(2)}) async-start(bf16[8,2,18432]{2,1,0:T(2,128)(2,1)} %reshape.406), calls=%async_computation | async-start | bytes 1179648 | tf_op jit(solution)/shard_map/all_to_all | solution.py:106
  29.7 5.9 %fusion = bf16[1,1,256,3456]{3,2,1,0:T(8,128)(2,1)S(1)} fusion(bf16[1152,3456]{1,0:T(8,128)(2,1)} %param.12, bf16[1,1,256,1152]{3,2,1,0:T(8,128)(2,1)S(1)} %copy-done.4, f32[1152]{0:T(1024)S(1)} %copy-done.26, f32[256]{0:T(256)S(1)} %fusion.57, f32[256]{0:T(256)S(1)} %broadcast_multiply_fusion.1), kind=kOutput, calls=%fused_computation.3 | convolution fusion | flops 2040791040 | bytes 10328576 | tf_op jit(solution)/shard_map/jvp()/dot_general | solution.py:19
  36.9 2.1 copy.73
  39.0 2.1 copy.72
  41.1 2.1 copy.71
  43.2 2.0 multiply_reduce_fusion.1
  47.4 2.4 convolution_convert_fusion.13
  52.0 2.7 fusion.1
  54.7 5.0 %copy.131 = bf16[1,1,256,3456]{3,1,0,2:T(2,128)(2,1)} copy(bf16[1,1,256,3456]{3,2,1,0:T(8,128)(2,1)S(1)} %fusion.1) | data formatting | bytes 3538944 | tf_op jit(solution)/shard_map/jvp()/convert_element_type | solution.py:95
  59.7 13.1 %reduce.22 = bf16[256,3456]{1,0:T(8,128)(2,1)} reduce(bf16[256,1,1,3456]{3,2,1,0:T(2,128)(2,1)} %bitcast.146, bf16[]{:T(256)} %broadcast.212), dimensions={1,2}, to_apply=%bitcast.144.reduce_sub_computation | reduce | bytes 3538946
  72.8 5.7 %reshape.404 = bf16[8,2,55296]{2,1,0:T(2,128)(2,1)} reshape(bf16[256,3456]{1,0:T(8,128)(2,1)} %reduce.22) | data formatting | bytes 3538944
  78.5 6.6 %all-to-all-start.1 = ((bf16[8,2,55296]{2,1,0:T(2,128)(2,1)}), bf16[8,2,55296]{2,1,0:T(2,128)(2,1)}, u32[]{:S(2)}, u32[]{:S(2)}) async-start(bf16[8,2,55296]{2,1,0:T(2,128)(2,1)} %reshape.404), calls=%async_computation.1 | async-start | bytes 3538944 | tf_op jit(solution)/shard_map/all_to_all | solution.py:100
  85.2 3.5 reshape.407
  88.7 5.5 %bitcast_reduce_fusion = bf16[256,1152]{1,0:T(8,128)(2,1)} fusion(bf16[256,1,1,1152]{3,2,1,0:T(2,128)(2,1)} %reshape.407), kind=kLoop, calls=%fused_computation.115 | loop fusion | bytes 1179648 | tf_op jit(solution)/shard_map/all_to_all | solution.py:106
  94.2 3.7 %reshape.381 = bf16[1,8,32,16,72]{4,3,2,1,0:T(8,128)(2,1)} reshape(bf16[256,1152]{1,0:T(8,128)(2,1)} %bitcast_reduce_fusion) | data formatting | bytes 1179648 | tf_op jit(solution)/shard_map/transpose(jvp())/reshape | solution.py:54
  97.9 9.9 %all-to-all-done.1 = bf16[8,2,55296]{2,1,0:T(2,128)(2,1)} async-done(((bf16[8,2,55296]{2,1,0:T(2,128)(2,1)}), bf16[8,2,55296]{2,1,0:T(2,128)(2,1)}, u32[]{:S(2)}, u32[]{:S(2)}) %all-to-all-start.1) | async-done | bytes 1769504 | tf_op jit(solution)/shard_map/all_to_all | solution.py:100
  107.9 6.5 %reshape.405 = bf16[256,1,1,3456]{3,2,1,0:T(2,128)(2,1)} reshape(bf16[8,2,55296]{2,1,0:T(2,128)(2,1)} %all-to-all-done.1) | data formatting | bytes 3538944
  114.4 2.2 copy.100
  117.9 3.7 %reshape.388 = bf16[8,32,16,72]{3,2,1,0:T(8,128)(2,1)} reshape(bf16[1,8,32,1152]{3,2,1,0:T(8,128)(2,1)} %get-tuple-element.4) | data formatting | bytes 1179648 | tf_op jit(solution)/shard_map/reshape.54
  121.6 3.7 %reshape.391 = bf16[8,32,16,72]{3,2,1,0:T(8,128)(2,1)} reshape(bf16[1,8,32,1152]{3,2,1,0:T(8,128)(2,1)} %get-tuple-element.5) | data formatting | bytes 1179648 | tf_op jit(solution)/shard_map/reshape.63
  125.3 3.9 %reshape.389 = bf16[8,32,16,72]{3,2,1,0:T(8,128)(2,1)} reshape(bf16[1,8,32,1152]{3,2,1,0:T(8,128)(2,1)} %get-tuple-element.6) | data formatting | bytes 1179648 | tf_op jit(solution)/shard_map/reshape.55
  129.2 3.2 multiply_reduce_fusion.3
  134.4 2.8 fusion.22
  137.2 2.3 multiply_reduce_fusion.2
  139.6 4.1 %fusion.21 = bf16[1,8,32,16,72]{4,1,3,2,0:T(8,128)(2,1)} fusion(bf16[8,32,16,72]{3,2,1,0:T(8,128)(2,1)S(1)} %copy-done.13, f32[32,16,8,8]{2,3,1,0:T(8,128)S(1)} %get-tuple-element.17, f32[32,16,8]{2,1,0:T(8,128)S(1)} %neg.20, f32[32,16,8]{2,1,0:T(8,128)S(1)} %fusion.56, f32[32,16,8]{2,1,0:T(8,128)S(1)} %get-tuple-element.14, ...), kind=kOutput, calls=%fused_computation.47 | convolution fusion | flops 28803072 | bytes 1490944 | tf_op jit(solution)/shard_map/transpose(jvp(bqphd,bkphd->bphqk))/dot_general | solution.py:49
  143.7 3.8 %fusion.20 = bf16[1,8,32,16,72]{4,1,3,2,0:T(8,128)(2,1)} fusion(bf16[8,32,16,72]{3,2,1,0:T(8,128)(2,1)S(1)} %copy-done.12, f32[32,16,8,8]{2,3,1,0:T(8,128)S(1)} %get-tuple-element.17, f32[32,16,8]{2,1,0:T(8,128)S(1)} %neg.20, f32[32,16,8]{2,1,0:T(8,128)S(1)} %fusion.56, f32[32,16,8]{2,1,0:T(8,128)S(1)} %get-tuple-element.14, ...), kind=kOutput, calls=%fused_computation.46 | convolution fusion | flops 28803072 | bytes 1490944 | tf_op jit(solution)/shard_map/transpose(jvp(bqphd,bkphd->bphqk))/dot_general | solution.py:49
  148.6 2.9 convert_element_type.198
  151.6 5.6 %all-to-all-start.3 = ((bf16[1,8,32,1152]{3,2,0,1:T(8,128)(2,1)}), bf16[1,8,32,1152]{3,2,0,1:T(8,128)(2,1)}, u32[]{:S(2)}, u32[]{:S(2)}) async-start(bf16[1,8,32,1152]{3,2,0,1:T(8,128)(2,1)} %bitcast.158), calls=%async_computation.3 | async-start | bytes 1179648 | tf_op jit(solution)/shard_map/all_to_all | solution.py:102
  157.1 4.6 %fusion.19 = bf16[1,8,32,16,72]{4,1,3,2,0:T(8,128)(2,1)S(1)} fusion(bf16[1,8,32,16,72]{4,3,2,1,0:T(8,128)(2,1)} %reshape.381, f32[32,16,8]{2,1,0:T(8,128)} %copy-done.19, f32[32,16,8,8]{2,3,1,0:T(8,128)} %copy-done.3, f32[32,16,8]{2,1,0:T(8,128)S(1)} %get-tuple-element.14), kind=kOutput, calls=%fused_computation.45 | convolution fusion | flops 28704768 | bytes 1343488 | tf_op jit(solution)/shard_map/transpose(jvp(bphqk,bkphd->bqphd))/dot_general | solution.py:53
  162.9 2.9 reshape.390
  165.8 2.3 copy.81
  168.1 2.9 reshape.392
  171.0 2.3 copy.84
  173.4 2.9 reshape.393
  176.3 2.8 add_bitcast_fusion
  179.1 6.6 %all-to-all-start.2 = ((bf16[1,8,32,3456]{3,2,0,1:T(8,128)(2,1)}), bf16[1,8,32,3456]{3,2,0,1:T(8,128)(2,1)}, u32[]{:S(2)}, u32[]{:S(2)}) async-start(bf16[1,8,32,3456]{3,2,0,1:T(8,128)(2,1)} %add_bitcast_fusion), calls=%async_computation.2 | async-start | bytes 3538944 | tf_op jit(solution)/shard_map/all_to_all | solution.py:108
  186.2 4.6 %convolution_multiply_fusion = f32[1152,1152]{1,0:T(8,128)} fusion(bf16[256,1152]{1,0:T(8,128)(2,1)} %bitcast.47, bf16[1,1,256,1152]{3,2,1,0:T(8,128)(2,1)} %param.9), kind=kOutput, calls=%fused_computation | convolution fusion | flops 680804352 | bytes 6488064 | tf_op jit(solution)/shard_map/dot_general | solution.py:65
  190.8 18.2 %all-to-all-done.2 = bf16[1,8,32,3456]{3,2,0,1:T(8,128)(2,1)} async-done(((bf16[1,8,32,3456]{3,2,0,1:T(8,128)(2,1)}), bf16[1,8,32,3456]{3,2,0,1:T(8,128)(2,1)}, u32[]{:S(2)}, u32[]{:S(2)}) %all-to-all-start.2) | async-done | bytes 1769504 | tf_op jit(solution)/shard_map/all_to_all | solution.py:108
  209.1 6.8 %fusion.28 = (f32[256]{0:T(256)S(1)}, f32[256,1152]{1,0:T(8,128)S(1)}) fusion(f32[1,1,256,1152]{3,2,1,0:T(8,128)} %copy-done.7, f32[256]{0:T(256)S(1)} %copy-done.21, f32[1152]{0:T(1024)S(1)} %copy-done.25, bf16[256,3456]{1,0:T(8,128)(2,1)} %bitcast.23, bf16[1152,3456]{1,0:T(8,128)(2,1)} %param.14), kind=kOutput, calls=%fused_computation.59 | convolution fusion | flops 2040200960 | bytes 12098048 | tf_op jit(solution)/shard_map/transpose(jvp())/dot_general | solution.py:19
  219.2 2.1 copy.86
  221.4 4.1 %multiply_reduce_fusion = (f32[16,256]{1,0:T(8,128)S(1)}, f32[16,256,256]{1,2,0:T(8,128)S(1)}) fusion(f32[16,256]{1,0:T(8,128)S(1)} %multiply_divide_fusion.1, f32[16,256]{1,0:T(8,128)S(1)} %get-tuple-element.10, f32[16,256,256]{1,2,0:T(8,128)} %copy-done.1, bf16[16,72,256]{2,1,0:T(8,128)(2,1)} %bitcast.156, bf16[256,16,72]{0,2,1:T(8,128)(2,1)} %bitcast.154), kind=kOutput, calls=%fused_computation.6 | convolution fusion | flops 156233728 | bytes 9617408 | tf_op jit(solution)/shard_map/transpose(jvp(bfhqk,bfkhd->bfqhd))/dot_general | solution.py:38
  228.5 2.3 convolution_convert_fusion.11
  230.8 3.1 convolution_convert_fusion.12
  233.9 2.8 fusion.26
  239.5 113.6 %all-reduce.9.cloned.1.call-done = f32[1152,1152]{1,0:T(8,128)} async-done(((f32[1152,1152]{1,0:T(8,128)}), f32[1152,1152]{1,0:T(8,128)}) %all-reduce.9.cloned.1.call-update) | async-done | bytes 5308432
  (101 shorter events, 25.3 us)
Async XLA Ops:
  7.2 42.6 %copy-start = (bf16[1152,1152]{1,0:T(8,128)(2,1)S(1)}, bf16[1152,1152]{1,0:T(8,128)(2,1)}, u32[]{:S(2)}) copy-start(bf16[1152,1152]{1,0:T(8,128)(2,1)} %param.13) | copy-start | bytes 7962628
  12.2 17.0 %copy-start.4 = (bf16[1,1,256,1152]{3,2,1,0:T(8,128)(2,1)S(1)}, bf16[1,1,256,1152]{3,2,1,0:T(8,128)(2,1)}, u32[]{:S(2)}) copy-start(bf16[1,1,256,1152]{3,2,1,0:T(8,128)(2,1)} %param.8) | copy-start | bytes 1769476
  18.9 10.8 %copy-start.26 = (f32[1152]{0:T(1024)S(1)}, f32[1152]{0:T(1024)}, u32[]{:S(2)}) copy-start(f32[1152]{0:T(1024)} %param.10) | copy-start | bytes 13828
  21.4 57.1 %all-to-all-start = ((bf16[8,2,18432]{2,1,0:T(2,128)(2,1)}), bf16[8,2,18432]{2,1,0:T(2,128)(2,1)}, u32[]{:S(2)}, u32[]{:S(2)}) async-start(bf16[8,2,18432]{2,1,0:T(2,128)(2,1)} %reshape.406), calls=%async_computation | async-start | bytes 1179648 | tf_op jit(solution)/shard_map/all_to_all | solution.py:106
  45.3 2.1 copy-start.1
  45.3 2.1 copy-start.15
  45.3 6.7 %slice-start = ((s8[7962624]{0:T(1024)(128)(4,1)}), s8[4194304]{0:T(1024)(128)(4,1)S(1)}, s32[]{:S(2)}) async-start(s8[7962624]{0:T(1024)(128)(4,1)} %bitcast.161), calls=%async_computation.5 | async-start | bytes 8388608
  47.4 4.6 %slice-start.1 = ((s8[7962624]{0:T(1024)(128)(4,1)}), s8[3768320]{0:T(1024)(128)(4,1)S(1)}, s32[]{:S(2)}) async-start(s8[7962624]{0:T(1024)(128)(4,1)} %bitcast.161), calls=%async_computation.6 | async-start | bytes 7536640
  49.8 2.2 copy-start.24
  51.0 1.0 copy-start.7
  51.0 3.7 %copy-start.20 = (f32[256]{0:T(256)}, f32[256]{0:T(256)S(1)}, u32[]{:S(2)}) copy-start(f32[256]{0:T(256)S(1)} %broadcast_multiply_fusion) | copy-start | bytes 3076
  52.0 2.7 copy-start.22
  78.5 29.3 %all-to-all-start.1 = ((bf16[8,2,55296]{2,1,0:T(2,128)(2,1)}), bf16[8,2,55296]{2,1,0:T(2,128)(2,1)}, u32[]{:S(2)}, u32[]{:S(2)}) async-start(bf16[8,2,55296]{2,1,0:T(2,128)(2,1)} %reshape.404), calls=%async_computation.1 | async-start | bytes 3538944 | tf_op jit(solution)/shard_map/all_to_all | solution.py:100
  132.4 11.3 %copy-start.3 = (f32[32,16,8,8]{2,3,1,0:T(8,128)}, f32[32,16,8,8]{2,3,1,0:T(8,128)S(1)}, u32[]{:S(2)}) copy-start(f32[32,16,8,8]{2,3,1,0:T(8,128)S(1)} %get-tuple-element.15) | copy-start | bytes 393220
  132.4 2.0 copy-start.14
  133.4 10.3 %copy-start.19 = (f32[32,16,8]{2,1,0:T(8,128)}, f32[32,16,8]{2,1,0:T(8,128)S(1)}, u32[]{:S(2)}) copy-start(f32[32,16,8]{2,1,0:T(8,128)S(1)} %fusion.56) | copy-start | bytes 49156
  134.4 2.8 copy-start.11
  137.2 2.3 copy-start.13
  139.6 4.1 %copy-start.12 = (bf16[8,32,16,72]{3,2,1,0:T(8,128)(2,1)S(1)}, bf16[8,32,16,72]{3,2,1,0:T(8,128)(2,1)}, u32[]{:S(2)}) copy-start(bf16[8,32,16,72]{3,2,1,0:T(8,128)(2,1)} %reshape.388) | copy-start | bytes 1769476
  151.6 27.5 %all-to-all-start.3 = ((bf16[1,8,32,1152]{3,2,0,1:T(8,128)(2,1)}), bf16[1,8,32,1152]{3,2,0,1:T(8,128)(2,1)}, u32[]{:S(2)}, u32[]{:S(2)}) async-start(bf16[1,8,32,1152]{3,2,0,1:T(8,128)(2,1)} %bitcast.158), calls=%async_computation.3 | async-start | bytes 1179648 | tf_op jit(solution)/shard_map/all_to_all | solution.py:102
  179.1 30.0 %all-to-all-start.2 = ((bf16[1,8,32,3456]{3,2,0,1:T(8,128)(2,1)}), bf16[1,8,32,3456]{3,2,0,1:T(8,128)(2,1)}, u32[]{:S(2)}, u32[]{:S(2)}) async-start(bf16[1,8,32,3456]{3,2,0,1:T(8,128)(2,1)} %add_bitcast_fusion), calls=%async_computation.2 | async-start | bytes 3538944 | tf_op jit(solution)/shard_map/all_to_all | solution.py:108
  185.7 167.4 %all-reduce.9.cloned.1.call-start = ((), (), s32[]{:S(2)}) async-start(), calls=%async_computation.4 | async-start | bytes 10616832
  190.8 18.3 %copy-start.21 = (f32[256]{0:T(256)S(1)}, f32[256]{0:T(256)}, u32[]{:S(2)}) copy-start(f32[256]{0:T(256)} %copy-done.20) | copy-start | bytes 3076
  190.8 18.3 %copy-start.25 = (f32[1152]{0:T(1024)S(1)}, f32[1152]{0:T(1024)}, u32[]{:S(2)}) copy-start(f32[1152]{0:T(1024)} %param.11) | copy-start | bytes 13828
  209.0 6.8 %copy-start.8 = (f32[1,1,256,1152]{3,2,1,0:T(8,128)S(1)}, f32[1,1,256,1152]{3,2,1,0:T(8,128)}, u32[]{:S(2)}) copy-start(f32[1,1,256,1152]{3,2,1,0:T(8,128)} %copy-done.7) | copy-start | bytes 3538948
  209.0 6.8 %copy-start.23 = (f32[256]{0:T(256)S(1)}, f32[256]{0:T(256)}, u32[]{:S(2)}) copy-start(f32[256]{0:T(256)} %copy-done.22) | copy-start | bytes 3076
  215.8 1.5 copy-start.17
  216.3 1.0 copy-start.9
  221.4 4.1 %copy-start.2 = (f32[16,256,256]{1,2,0:T(8,128)S(1)}, f32[16,256,256]{1,2,0:T(8,128)}, u32[]{:S(2)}) copy-start(f32[16,256,256]{1,2,0:T(8,128)} %copy-done.1) | copy-start | bytes 12582916
  225.5 1.2 copy-start.5
  226.7 1.8 copy-start.6
  228.5 2.3 copy-start.16
  228.5 5.4 %slice-start.2 = ((s8[7962624]{0:T(1024)(128)(4,1)}), s8[3768320]{0:T(1024)(128)(4,1)S(1)}, s32[]{:S(2)}) async-start(s8[7962624]{0:T(1024)(128)(4,1)} %bitcast.163), calls=%async_computation.7 | async-start | bytes 7536640
  230.8 3.1 slice-start.3
  230.8 3.1 copy-start.27
  236.7 1.3 copy-start.10
  236.8 1.4 copy-start.18
Sparse Core Ops, SparseCore 0:
  191.5 161.5 all-reduce.8
where the time goes:
time: 368 us; the launch traced here: 362 us
  waiting for transfers between devices  142 us (39%)
  local copies, waits for them, and re-layouts  84.9 us (23%)
  matrix products  65.4 us (18%)
  other arithmetic  27.8 us (8%)
  starting transfers between devices  27.1 us (7%)
  between operations  14.7 us (4%)
    unnamed x2, waiting for transfers between devices  114 us
    unnamed x71, local copies, waits for them, and re-layouts  27.9 us
    dot_general x7, matrix products, project(): return jnp.dot(hidden, weight, preferred_element_type=jnp.float32)  24.4 us
    unnamed x4, other arithmetic  19.1 us
    all_to_all x1, waiting for transfers between devices, per_device(): lax.all_to_all(qkv_grad_pos, 'seq', split_axis=1, concat_axis=2, tiled=True)  18.2 us
    another operation x3, local copies, waits for them, and re-layouts  11.3 us
    dot_general x3, matrix products, temporal_mix(): jnp.einsum('bqphd,bkphd->bphqk', query_part, key_part, precision=lax.Prec...  11.1 us
    all_to_all x1, waiting for transfers between devices, per_device(): lax.all_to_all(qkv, 'seq', split_axis=2, concat_axis=1, tiled=True)  9.94 us
  transfers between devices with their start and end apart: 5, of which 3 were waited for; matrix products, arithmetic and copies ran while one was open for 32% of the time, Pallas kernels for 0%

commit v1 on v0

--- a/solution.py
+++ b/solution.py
@@ -6,6 +6,13 @@
 
 HEADS = 16
 epsilon = 1e-06
+
+
+def stacked_exchange(value, name, split, join):
+    n_dev = lax.axis_size(name)
+    parts = jnp.stack(jnp.split(value, n_dev, axis=split), axis=0)
+    parts = lax.all_to_all(parts, name, split_axis=0, concat_axis=0)
+    return jnp.concatenate(parts, axis=join)
 
 
 def layer_norm(stream, gain_vec):
@@ -105,7 +112,7 @@
     mixed_grad = out_back(grad_float)[0]
     mixed_grad_pos = lax.all_to_all(mixed_grad, "seq", split_axis=2, concat_axis=1, tiled=True)
     qkv_grad_pos = mix_back(mixed_grad_pos)[0]
-    qkv_grad = lax.all_to_all(qkv_grad_pos, "seq", split_axis=1, concat_axis=2, tiled=True)
+    qkv_grad = stacked_exchange(qkv_grad_pos, "seq", 1, 2)
     stream_grad = grad_float + pre_back(qkv_grad)[0]
     video_grad = spatial_back(stream_grad)[0]
     local_sum = local_sum / math.sqrt(float(token_total))

time: 368 us -> 371 us (level)
  local copies, waits for them, and re-layouts: 84.9 us -> 90.9 us
    unnamed x71 -> x62, local copies, waits for them, and re-layouts: 27.9 us -> 31.9 us
    another operation x3 -> x4, local copies, waits for them, and re-layouts: 11.3 us -> 12 us
where the time goes in v1:
time: 371 us; the launch traced here: 365 us
  waiting for transfers between devices  142 us (38%)
  local copies, waits for them, and re-layouts  90.9 us (25%)
  matrix products  64.3 us (17%)
  starting transfers between devices  26.7 us (7%)
  other arithmetic  26.4 us (7%)
  between operations  14.6 us (4%)
    unnamed x2, waiting for transfers between devices  114 us
    unnamed x62, local copies, waits for them, and re-layouts  31.9 us
    dot_general x7, matrix products, project(): return jnp.dot(hidden, weight, preferred_element_type=jnp.float32)  24.4 us
    unnamed x4, other arithmetic  19 us
    all_to_all x1, waiting for transfers between devices, stacked_exchange(): parts = lax.all_to_all(parts, name, split_axis=0, concat_axis=0)  18.3 us
    another operation x3, local copies, waits for them, and re-layouts  11.2 us
    dot_general x3, matrix products, temporal_mix(): jnp.einsum('bqphd,bkphd->bphqk', query_part, key_part, precision=lax.Prec...  11.1 us
    all_to_all x1, waiting for transfers between devices, per_device(): lax.all_to_all(qkv, 'seq', split_axis=2, concat_axis=1, tiled=True)  9.96 us
  transfers between devices with their start and end apart: 5, of which 3 were waited for; matrix products, arithmetic and copies ran while one was open for 32% of the time, Pallas kernels for 0%

profile of v1, /device:TPU:1, one launch (start us, length us, event | category | flops | bytes accessed | tf_op | source)
XLA Modules:
  0.0 365.0 jit_solution(17450298150345353612)
XLA Ops:
  7.2 3.1 fusion.7
  12.7 6.0 %reduce.23 = bf16[256,1152]{1,0:T(8,128)(2,1)} reduce(bf16[256,1,1,1152]{3,2,1,0:T(2,128)(2,1)} %bitcast.183, bf16[]{:T(256)} %broadcast.212), dimensions={1,2}, to_apply=%bitcast.175.reduce_sub_computation | reduce | bytes 1179650
  18.7 2.6 reshape.404
  21.3 7.7 %all-to-all-start = ((bf16[8,2,18432]{2,1,0:T(2,128)(2,1)}), bf16[8,2,18432]{2,1,0:T(2,128)(2,1)}, u32[]{:S(2)}, u32[]{:S(2)}) async-start(bf16[8,2,18432]{2,1,0:T(2,128)(2,1)} %reshape.404), calls=%async_computation | async-start | bytes 1179648 | tf_op jit(solution)/shard_map/all_to_all | solution.py:113
  29.5 5.9 %fusion = bf16[1,1,256,3456]{3,2,1,0:T(8,128)(2,1)S(1)} fusion(bf16[1152,3456]{1,0:T(8,128)(2,1)} %param.12, bf16[1,1,256,1152]{3,2,1,0:T(8,128)(2,1)S(1)} %copy-done.3, f32[1152]{0:T(1024)S(1)} %copy-done.19, f32[256]{0:T(256)S(1)} %fusion.65, f32[256]{0:T(256)S(1)} %broadcast_multiply_fusion.1), kind=kOutput, calls=%fused_computation.3 | convolution fusion | flops 2040791040 | bytes 10328576 | tf_op jit(solution)/shard_map/jvp()/dot_general | solution.py:26
  36.7 2.1 copy.72
  38.9 2.1 copy.71
  41.0 2.1 copy.70
  43.1 2.0 multiply_reduce_fusion.1
  47.3 2.4 convolution_convert_fusion.13
  51.9 2.7 fusion.1
  54.6 5.0 %copy.129 = bf16[1,1,256,3456]{3,1,0,2:T(2,128)(2,1)} copy(bf16[1,1,256,3456]{3,2,1,0:T(8,128)(2,1)S(1)} %fusion.1) | data formatting | bytes 3538944 | tf_op jit(solution)/shard_map/jvp()/convert_element_type | solution.py:102
  59.6 13.0 %reduce.22 = bf16[256,3456]{1,0:T(8,128)(2,1)} reduce(bf16[256,1,1,3456]{3,2,1,0:T(2,128)(2,1)} %bitcast.176, bf16[]{:T(256)} %broadcast.212), dimensions={1,2}, to_apply=%bitcast.174.reduce_sub_computation | reduce | bytes 3538946
  72.6 5.7 %reshape.402 = bf16[8,2,55296]{2,1,0:T(2,128)(2,1)} reshape(bf16[256,3456]{1,0:T(8,128)(2,1)} %reduce.22) | data formatting | bytes 3538944
  78.3 6.6 %all-to-all-start.1 = ((bf16[8,2,55296]{2,1,0:T(2,128)(2,1)}), bf16[8,2,55296]{2,1,0:T(2,128)(2,1)}, u32[]{:S(2)}, u32[]{:S(2)}) async-start(bf16[8,2,55296]{2,1,0:T(2,128)(2,1)} %reshape.402), calls=%async_computation.1 | async-start | bytes 3538944 | tf_op jit(solution)/shard_map/all_to_all | solution.py:107
  84.9 3.5 reshape.405
  88.5 5.5 %bitcast_reduce_fusion = bf16[256,1152]{1,0:T(8,128)(2,1)} fusion(bf16[256,1,1,1152]{3,2,1,0:T(2,128)(2,1)} %reshape.405), kind=kLoop, calls=%fused_computation.131 | loop fusion | bytes 1179648 | tf_op jit(solution)/shard_map/all_to_all | solution.py:113
  94.0 3.7 %reshape.379 = bf16[1,8,32,16,72]{4,3,2,1,0:T(8,128)(2,1)} reshape(bf16[256,1152]{1,0:T(8,128)(2,1)} %bitcast_reduce_fusion) | data formatting | bytes 1179648 | tf_op jit(solution)/shard_map/transpose(jvp())/reshape | solution.py:61
  97.7 10.0 %all-to-all-done.1 = bf16[8,2,55296]{2,1,0:T(2,128)(2,1)} async-done(((bf16[8,2,55296]{2,1,0:T(2,128)(2,1)}), bf16[8,2,55296]{2,1,0:T(2,128)(2,1)}, u32[]{:S(2)}, u32[]{:S(2)}) %all-to-all-start.1) | async-done | bytes 1769504 | tf_op jit(solution)/shard_map/all_to_all | solution.py:107
  107.6 6.5 %reshape.403 = bf16[256,1,1,3456]{3,2,1,0:T(2,128)(2,1)} reshape(bf16[8,2,55296]{2,1,0:T(2,128)(2,1)} %all-to-all-done.1) | data formatting | bytes 3538944
  114.2 2.2 copy.98
  117.7 3.7 %reshape.386 = bf16[8,32,16,72]{3,2,1,0:T(8,128)(2,1)} reshape(bf16[1,8,32,1152]{3,2,1,0:T(8,128)(2,1)} %get-tuple-element.4) | data formatting | bytes 1179648 | tf_op jit(solution)/shard_map/reshape.55
  121.4 3.7 %reshape.389 = bf16[8,32,16,72]{3,2,1,0:T(8,128)(2,1)} reshape(bf16[1,8,32,1152]{3,2,1,0:T(8,128)(2,1)} %get-tuple-element.5) | data formatting | bytes 1179648 | tf_op jit(solution)/shard_map/reshape.64
  125.1 3.9 %reshape.387 = bf16[8,32,16,72]{3,2,1,0:T(8,128)(2,1)} reshape(bf16[1,8,32,1152]{3,2,1,0:T(8,128)(2,1)} %get-tuple-element.6) | data formatting | bytes 1179648 | tf_op jit(solution)/shard_map/reshape.56
  128.9 3.2 multiply_reduce_fusion.3
  133.4 2.8 fusion.22
  136.2 3.6 fusion.19
  139.8 2.3 multiply_reduce_fusion.2
  142.1 4.1 %fusion.21 = bf16[1,8,32,16,72]{4,1,3,2,0:T(8,128)(2,1)} fusion(bf16[8,32,16,72]{3,2,1,0:T(8,128)(2,1)S(1)} %copy-done.12, f32[32,16,8,8]{2,3,1,0:T(8,128)S(1)} %get-tuple-element.17, f32[32,16,8]{2,1,0:T(8,128)S(1)} %neg.20, f32[32,16,8]{2,1,0:T(8,128)S(1)} %fusion.64, f32[32,16,8]{2,1,0:T(8,128)S(1)} %get-tuple-element.14, ...), kind=kOutput, calls=%fused_computation.47 | convolution fusion | flops 28803072 | bytes 1490944 | tf_op jit(solution)/shard_map/transpose(jvp(bqphd,bkphd->bphqk))/dot_general | solution.py:56
  146.2 3.8 %fusion.20 = bf16[1,8,32,16,72]{4,1,3,2,0:T(8,128)(2,1)} fusion(bf16[8,32,16,72]{3,2,1,0:T(8,128)(2,1)S(1)} %copy-done.11, f32[32,16,8,8]{2,3,1,0:T(8,128)S(1)} %get-tuple-element.17, f32[32,16,8]{2,1,0:T(8,128)S(1)} %neg.20, f32[32,16,8]{2,1,0:T(8,128)S(1)} %fusion.64, f32[32,16,8]{2,1,0:T(8,128)S(1)} %get-tuple-element.14, ...), kind=kOutput, calls=%fused_computation.46 | convolution fusion | flops 28803072 | bytes 1490944 | tf_op jit(solution)/shard_map/transpose(jvp(bqphd,bkphd->bphqk))/dot_general | solution.py:56
  151.2 2.9 convert_element_type.198
  154.1 5.2 %all-to-all-start.3 = ((bf16[1,8,32,1152]{3,2,0,1:T(8,128)(2,1)}), bf16[1,8,32,1152]{3,2,0,1:T(8,128)(2,1)}, u32[]{:S(2)}, u32[]{:S(2)}) async-start(bf16[1,8,32,1152]{3,2,0,1:T(8,128)(2,1)} %bitcast.188), calls=%async_computation.3 | async-start | bytes 1179648 | tf_op jit(solution)/shard_map/all_to_all | solution.py:109
  159.3 2.4 copy.77
  161.7 2.9 reshape.388
  164.6 2.3 copy.80
  166.9 2.9 reshape.390
  169.8 2.3 copy.83
  172.2 2.9 reshape.391
  182.3 6.6 %all-to-all-start.2 = ((bf16[8,1,1,32,3456]{4,3,2,1,0:T(8,128)(2,1)}), bf16[8,1,1,32,3456]{4,3,2,1,0:T(8,128)(2,1)}, u32[]{:S(2)}, u32[]{:S(2)}) async-start(bf16[8,1,1,32,3456]{4,3,2,1,0:T(8,128)(2,1)} %fusion.56), calls=%async_computation.2 | async-start | bytes 3538944 | tf_op jit(solution)/shard_map/all_to_all | solution.py:14
  189.5 4.5 %convolution_multiply_fusion = f32[1152,1152]{1,0:T(8,128)} fusion(bf16[256,1152]{1,0:T(8,128)(2,1)} %bitcast.54, bf16[1,1,256,1152]{3,2,1,0:T(8,128)(2,1)} %param.9), kind=kOutput, calls=%fused_computation | convolution fusion | flops 680804352 | bytes 6488064 | tf_op jit(solution)/shard_map/dot_general | solution.py:72
  194.0 18.3 %all-to-all-done.2 = bf16[8,1,1,32,3456]{4,3,2,1,0:T(8,128)(2,1)} async-done(((bf16[8,1,1,32,3456]{4,3,2,1,0:T(8,128)(2,1)}), bf16[8,1,1,32,3456]{4,3,2,1,0:T(8,128)(2,1)}, u32[]{:S(2)}, u32[]{:S(2)}) %all-to-all-start.2) | async-done | bytes 1769504 | tf_op jit(solution)/shard_map/all_to_all | solution.py:14
  212.3 6.8 %fusion.28 = (f32[256]{0:T(256)S(1)}, f32[256,1152]{1,0:T(8,128)S(1)}) fusion(f32[1,1,256,1152]{3,2,1,0:T(8,128)} %copy-done.6, f32[256]{0:T(256)S(1)} %broadcast_multiply_fusion, f32[1152]{0:T(1024)S(1)} %copy-done.18, bf16[256,3456]{1,0:T(8,128)(2,1)} %bitcast.30, bf16[1152,3456]{1,0:T(8,128)(2,1)} %param.14), kind=kOutput, calls=%fused_computation.59 | convolution fusion | flops 2040200960 | bytes 12098048 | tf_op jit(solution)/shard_map/transpose(jvp())/dot_general | solution.py:26
  222.5 2.2 copy.84
  224.6 4.1 %multiply_reduce_fusion = (f32[16,256]{1,0:T(8,128)S(1)}, f32[16,256,256]{1,2,0:T(8,128)S(1)}) fusion(f32[16,256]{1,0:T(8,128)S(1)} %multiply_divide_fusion.1, f32[16,256]{1,0:T(8,128)S(1)} %get-tuple-element.10, f32[16,256,256]{1,2,0:T(8,128)} %copy-done.1, bf16[16,72,256]{2,1,0:T(8,128)(2,1)} %bitcast.186, bf16[256,16,72]{0,2,1:T(8,128)(2,1)} %bitcast.184), kind=kOutput, calls=%fused_computation.6 | convolution fusion | flops 156233728 | bytes 9617408 | tf_op jit(solution)/shard_map/transpose(jvp(bfhqk,bfkhd->bfqhd))/dot_general | solution.py:45
  231.8 2.3 convolution_convert_fusion.11
  234.1 3.1 convolution_convert_fusion.12
  237.2 2.8 fusion.26
  242.8 113.7 %all-reduce.9.cloned.1.call-done = f32[1152,1152]{1,0:T(8,128)} async-done(((f32[1152,1152]{1,0:T(8,128)}), f32[1152,1152]{1,0:T(8,128)}) %all-reduce.9.cloned.1.call-update) | async-done | bytes 5308432
  (93 shorter events, 30.4 us)
Async XLA Ops:
  7.2 42.5 %copy-start = (bf16[1152,1152]{1,0:T(8,128)(2,1)S(1)}, bf16[1152,1152]{1,0:T(8,128)(2,1)}, u32[]{:S(2)}) copy-start(bf16[1152,1152]{1,0:T(8,128)(2,1)} %param.13) | copy-start | bytes 7962628
  12.2 16.8 %copy-start.3 = (bf16[1,1,256,1152]{3,2,1,0:T(8,128)(2,1)S(1)}, bf16[1,1,256,1152]{3,2,1,0:T(8,128)(2,1)}, u32[]{:S(2)}) copy-start(bf16[1,1,256,1152]{3,2,1,0:T(8,128)(2,1)} %param.8) | copy-start | bytes 1769476
  18.7 10.8 %copy-start.19 = (f32[1152]{0:T(1024)S(1)}, f32[1152]{0:T(1024)}, u32[]{:S(2)}) copy-start(f32[1152]{0:T(1024)} %param.10) | copy-start | bytes 13828
  21.3 57.0 %all-to-all-start = ((bf16[8,2,18432]{2,1,0:T(2,128)(2,1)}), bf16[8,2,18432]{2,1,0:T(2,128)(2,1)}, u32[]{:S(2)}, u32[]{:S(2)}) async-start(bf16[8,2,18432]{2,1,0:T(2,128)(2,1)} %reshape.404), calls=%async_computation | async-start | bytes 1179648 | tf_op jit(solution)/shard_map/all_to_all | solution.py:113
  45.1 2.1 copy-start.1
  45.1 2.1 copy-start.14
  45.1 6.7 %slice-start = ((s8[7962624]{0:T(1024)(128)(4,1)}), s8[4194304]{0:T(1024)(128)(4,1)S(1)}, s32[]{:S(2)}) async-start(s8[7962624]{0:T(1024)(128)(4,1)} %bitcast.191), calls=%async_computation.5 | async-start | bytes 8388608
  47.3 4.6 %slice-start.1 = ((s8[7962624]{0:T(1024)(128)(4,1)}), s8[3768320]{0:T(1024)(128)(4,1)S(1)}, s32[]{:S(2)}) async-start(s8[7962624]{0:T(1024)(128)(4,1)} %bitcast.191), calls=%async_computation.6 | async-start | bytes 7536640
  49.7 2.2 copy-start.18
  50.8 1.0 copy-start.6
  78.3 29.4 %all-to-all-start.1 = ((bf16[8,2,55296]{2,1,0:T(2,128)(2,1)}), bf16[8,2,55296]{2,1,0:T(2,128)(2,1)}, u32[]{:S(2)}, u32[]{:S(2)}) async-start(bf16[8,2,55296]{2,1,0:T(2,128)(2,1)} %reshape.402), calls=%async_computation.1 | async-start | bytes 3538944 | tf_op jit(solution)/shard_map/all_to_all | solution.py:107
  132.1 1.2 copy-start.13
  133.4 2.8 copy-start.10
  139.8 2.3 copy-start.12
  142.1 4.1 %copy-start.11 = (bf16[8,32,16,72]{3,2,1,0:T(8,128)(2,1)S(1)}, bf16[8,32,16,72]{3,2,1,0:T(8,128)(2,1)}, u32[]{:S(2)}) copy-start(bf16[8,32,16,72]{3,2,1,0:T(8,128)(2,1)} %reshape.386) | copy-start | bytes 1769476
  154.1 28.2 %all-to-all-start.3 = ((bf16[1,8,32,1152]{3,2,0,1:T(8,128)(2,1)}), bf16[1,8,32,1152]{3,2,0,1:T(8,128)(2,1)}, u32[]{:S(2)}, u32[]{:S(2)}) async-start(bf16[1,8,32,1152]{3,2,0,1:T(8,128)(2,1)} %bitcast.188), calls=%async_computation.3 | async-start | bytes 1179648 | tf_op jit(solution)/shard_map/all_to_all | solution.py:109
  182.3 30.0 %all-to-all-start.2 = ((bf16[8,1,1,32,3456]{4,3,2,1,0:T(8,128)(2,1)}), bf16[8,1,1,32,3456]{4,3,2,1,0:T(8,128)(2,1)}, u32[]{:S(2)}, u32[]{:S(2)}) async-start(bf16[8,1,1,32,3456]{4,3,2,1,0:T(8,128)(2,1)} %fusion.56), calls=%async_computation.2 | async-start | bytes 3538944 | tf_op jit(solution)/shard_map/all_to_all | solution.py:14
  189.0 167.4 %all-reduce.9.cloned.1.call-start = ((), (), s32[]{:S(2)}) async-start(), calls=%async_computation.4 | async-start | bytes 10616832
  212.3 6.8 %copy-start.7 = (f32[1,1,256,1152]{3,2,1,0:T(8,128)S(1)}, f32[1,1,256,1152]{3,2,1,0:T(8,128)}, u32[]{:S(2)}) copy-start(f32[1,1,256,1152]{3,2,1,0:T(8,128)} %copy-done.6) | copy-start | bytes 3538948
  219.1 1.5 copy-start.16
  219.5 1.0 copy-start.8
  224.6 4.1 %copy-start.2 = (f32[16,256,256]{1,2,0:T(8,128)S(1)}, f32[16,256,256]{1,2,0:T(8,128)}, u32[]{:S(2)}) copy-start(f32[16,256,256]{1,2,0:T(8,128)} %copy-done.1) | copy-start | bytes 12582916
  228.8 1.2 copy-start.4
  230.0 1.8 copy-start.5
  231.8 2.3 copy-start.15
  231.8 5.4 %slice-start.2 = ((s8[7962624]{0:T(1024)(128)(4,1)}), s8[3768320]{0:T(1024)(128)(4,1)S(1)}, s32[]{:S(2)}) async-start(s8[7962624]{0:T(1024)(128)(4,1)} %bitcast.193), calls=%async_computation.7 | async-start | bytes 7536640
  234.1 3.1 slice-start.3
  240.0 1.3 copy-start.9
  240.0 1.4 copy-start.17
Sparse Core Ops, SparseCore 0:
  194.7 161.6 all-reduce.8
